TPU v7x, 128 devices: a whole 4x4x4 slice. The times are simulated.
128 devices in a mesh: wide: 8 (over x, core), rep: 16 (over y, z).
Axes of the slice: x: 4, y: 4, z: 4, core: 2. Of those that a mesh axis runs over, the one named last changes fastest.
Arguments:
- stretch_qkv: bfloat16 [16, 1536, 3, 5120], P('rep', 'wide'), may hold values from -60 to 60
- norm_gains: float32 [2, 5120], replicated, may hold values from 0.25 to 1.75
- cache: bfloat16 [256, 2, 192, 5120], P('rep', None, 'wide'), may hold values from -6 to 6
- cached_stretches: int32 [16], replicated, may hold values from 1 to 2, as said below
- block_slot: int32 [16, 16], replicated, may hold values from 0 to 255, as said below
- video_of_group: int32 [16], replicated, may hold values from 0 to 15, each once
Outputs:
- attended: bfloat16 [16, 1536, 5120], P('rep', 'wide')
Inputs may be any that keep to these rules, and one draw needn't show every extreme that they name: `cached_stretches`: each value is 1 to 2; some video has exactly 2. Block b of video u holds that video's cached tokens b * 192 to (b + 1) * 192 - 1, oldest first; it is cache row block_slot[u, b], owned by group block_slot[u, b] // 16. Every group owns exactly 1 block of every video; no two blocks share a row.
All inputs are finite; a program needn't handle non-finite values.
Results may differ from a plain program's by a relative error of at most 0.011.
Values may be sent and summed in bfloat16 or wider, within the bound.
A program may use at most 128 MiB of HBM per device.

v0:
```python
import math
import jax
import jax.numpy as jnp
from jax import lax
from jax.sharding import PartitionSpec as P

HD = 128
epsilon = 1e-06


def normalize(stretch_rows, gains_row):
    widened = stretch_rows.astype(jnp.float32)
    mean_square = jnp.mean(widened * widened, axis=-1, keepdims=True)
    return (widened * lax.rsqrt(mean_square + epsilon) * gains_row).astype(jnp.bfloat16)


def attend_block(query_rows, all_keys, all_values, usable):
    scores = jnp.einsum(
        "qhd,khd->hqk", query_rows, all_keys, preferred_element_type=jnp.float32
    ) * HD ** (-0.5)
    scores = jnp.where(usable[None, None, :], scores, -jnp.inf)
    row_max = jnp.max(scores, axis=-1, keepdims=True)
    weights = jnp.exp(scores - row_max)
    row_total = jnp.sum(weights, axis=-1, keepdims=True)
    mixed = jnp.einsum(
        "hqk,khd->qhd", weights.astype(jnp.bfloat16), all_values, preferred_element_type=jnp.float32
    )
    return (mixed / jnp.transpose(row_total, (1, 0, 2))).astype(jnp.bfloat16)


def body(stretch_qkv, norm_gains, cache, cached_stretches, block_slot, video_of_group):
    rep_count = lax.axis_size("rep")
    wide_count = lax.axis_size("wide")
    own_group = lax.axis_index("rep")
    stretch_rows = stretch_qkv[0]
    width = stretch_rows.shape[-1]
    head_width = width // wide_count
    heads_dev = head_width // HD
    queries = normalize(stretch_rows[:, 0], norm_gains[0])
    keys_new = normalize(stretch_rows[:, 1], norm_gains[1])
    framed = jnp.stack([queries, keys_new, stretch_rows[:, 2]], axis=1)
    headed = lax.all_to_all(framed, "wide", split_axis=2, concat_axis=0, tiled=True)
    stretch_len = headed.shape[0]
    slots_dev = cache.shape[0]
    cap_dev = slots_dev // rep_count
    blocks = block_slot.shape[1]
    block_wide = cache.shape[2]
    block_len = block_wide * wide_count
    group_ids = jnp.arange(rep_count, dtype=jnp.int32)
    pick_video = (video_of_group[:, None] == group_ids[None, :]).astype(jnp.int32)
    slot_table = jnp.dot(pick_video, block_slot)
    owned_here = (slot_table // slots_dev == own_group).astype(jnp.int32)
    rank_in_owner = jnp.cumsum(owned_here, axis=1) - owned_here
    local_slot = slot_table % slots_dev
    chosen = jnp.stack([jnp.sum(owned_here * (rank_in_owner == 0) * local_slot, axis=1)], axis=1)
    outgoing = cache[chosen.reshape(-1)].reshape((rep_count, cap_dev) + cache.shape[1:])
    split_heads = outgoing.reshape(rep_count, cap_dev, 2, block_wide, wide_count, head_width)
    moved = jnp.moveaxis(split_heads, 4, 0).reshape(
        wide_count * rep_count, cap_dev, 2, block_wide, head_width
    )
    received = lax.all_to_all(moved, ("wide", "rep"), split_axis=0, concat_axis=0, tiled=True)
    received = received.reshape(wide_count, rep_count, cap_dev, 2, block_wide, head_width)
    arrived = jnp.transpose(received, (1, 2, 3, 0, 4, 5)).reshape(
        rep_count, cap_dev, 2, block_len, head_width
    )
    is_me = (group_ids == own_group).astype(jnp.int32)
    own_table = jnp.sum(slot_table * is_me[:, None], axis=0)
    own_video = jnp.sum(video_of_group * is_me)
    own_count = jnp.sum(cached_stretches * (group_ids == own_video).astype(jnp.int32))
    owners = own_table // slots_dev
    block_order = jnp.arange(blocks, dtype=jnp.int32)
    before = jnp.sum(
        (
            (owners[:, None] == owners[None, :]) & (block_order[:, None] > block_order[None, :])
        ).astype(jnp.int32),
        axis=1,
    )
    flat_index = owners * cap_dev + before
    history = arrived.reshape((rep_count * cap_dev,) + arrived.shape[2:])[flat_index]
    hist_span = blocks * block_len
    hist_keys = history[:, 0].reshape(hist_span, heads_dev, HD)
    hist_values = history[:, 1].reshape(hist_span, heads_dev, HD)
    new_queries = headed[:, 0].reshape(stretch_len, heads_dev, HD)
    new_keys = headed[:, 1].reshape(stretch_len, heads_dev, HD)
    new_values = headed[:, 2].reshape(stretch_len, heads_dev, HD)
    query_block = math.gcd(stretch_len, 256)
    blocks_q = new_queries.reshape(stretch_len // query_block, query_block, heads_dev, HD)
    all_keys = jnp.concatenate([hist_keys, new_keys], axis=0)
    all_values = jnp.concatenate([hist_values, new_values], axis=0)
    key_position = jnp.arange(hist_span + stretch_len, dtype=jnp.int32)
    usable = (key_position < own_count * stretch_len) | (key_position >= hist_span)
    attended = lax.map(lambda piece: attend_block(piece, all_keys, all_values, usable), blocks_q)
    attended = attended.reshape(stretch_len, head_width)
    returned = lax.all_to_all(attended, "wide", split_axis=0, concat_axis=1, tiled=True)
    return returned[None]


def solution(mesh):
    in_specs = (P("rep", "wide", None, None), P(), P("rep", None, "wide", None), P(), P(), P())
    out_specs = P("rep", "wide", None)
    return jax.shard_map(body, mesh=mesh, in_specs=in_specs, out_specs=out_specs, check_vma=False)
```

profile of v0, /device:TPU:8, one launch (start us, length us, event | category | flops | bytes accessed | tf_op | source)
XLA Modules:
  0.0 599.3 jit_solution(7813864269104856117)
XLA Ops:
  9.2 15.6 %copy.77 = bf16[192,3,5120]{0,1,2:T(4,128)(2,1)} copy(bf16[192,3,5120]{2,0,1:T(8,128)(2,1)} %pad_maximum_fusion) | data formatting | bytes 11796480 | tf_op jit(solution)/shard_map/stack | solution.py:41
  47.8 99.4 %all-to-all-done = bf16[192,3,5120]{0,1,2:T(4,128)(2,1)} async-done(((bf16[192,3,5120]{0,1,2:T(4,128)(2,1)}), bf16[192,3,5120]{0,1,2:T(4,128)(2,1)}, u32[]{:S(2)}, u32[]{:S(2)}) %all-to-all-start) | async-done | bytes 5898272 | tf_op jit(solution)/shard_map/all_to_all | solution.py:42
  147.1 9.0 %all-to-all-start.1 = ((bf16[128,1,2,24,640]{4,3,2,1,0:T(8,128)(2,1)}), bf16[128,1,2,24,640]{4,3,2,1,0:T(8,128)(2,1)}, u32[]{:S(2)}, u32[]{:S(2)}) async-start(bf16[128,1,2,24,640]{4,3,2,1,0:T(8,128)(2,1)} %bitcast.97), calls=%async_computation.1 | async-start | bytes 15728640 | tf_op jit(solution)/shard_map/all_to_all | solution.py:61
  159.1 15.7 %copy.94 = bf16[192,3,8,640]{3,0,2,1:T(8,128)(2,1)} copy(bf16[192,3,8,640]{0,1,3,2:T(4,128)(2,1)} %bitcast.3) | data formatting | bytes 11796480 | tf_op jit(solution)/shard_map/all_to_all | solution.py:42
  192.4 66.4 %all-to-all-done.1 = bf16[128,1,2,24,640]{4,3,2,1,0:T(8,128)(2,1)} async-done(((bf16[128,1,2,24,640]{4,3,2,1,0:T(8,128)(2,1)}), bf16[128,1,2,24,640]{4,3,2,1,0:T(8,128)(2,1)}, u32[]{:S(2)}, u32[]{:S(2)}) %all-to-all-start.1) | async-done | bytes 7864352 | tf_op jit(solution)/shard_map/all_to_all | solution.py:61
  266.5 8.0 %gather_fusion.1 = bf16[16,2,192,640]{3,2,1,0:T(8,128)(2,1)} fusion(bf16[16,2,192,640]{3,2,1,0:T(8,128)(2,1)} %bitcast.95, s32[1024]{0:T(1024)S(1)} %pad_clamp_fusion), kind=kCustom, calls=%fused_computation.1 | custom fusion | bytes 15728704 | tf_op jit(solution)/shard_map/gather | solution.py:79
  280.1 8.5 %copy.84 = bf16[16,1,192,640]{2,0,3,1:T(8,128)(2,1)} copy(bf16[16,1,192,640]{3,2,1,0:T(8,128)(2,1)} %get-tuple-element.108) | data formatting | bytes 7864320 | tf_op jit(solution)/shard_map/slice | solution.py:81
  288.7 9.9 %reshape_squeeze.12 = bf16[3072,5,128]{0,2,1:T(8,128)(2,1)} reshape(bf16[16,1,192,640]{2,0,3,1:T(8,128)(2,1)} %copy.84) | data formatting | bytes 7864320 | tf_op jit(solution)/shard_map/reshape;squeeze | solution.py:81
  303.6 8.9 %copy.89 = bf16[4608,5,128]{2,0,1:T(8,128)(2,1)} copy(bf16[4608,5,128]{0,2,1:T(8,128)(2,1)} %pad_maximum_fusion.1) | data formatting | bytes 11796480
  312.4 8.5 %copy.86 = bf16[16,1,192,640]{2,0,3,1:T(8,128)(2,1)} copy(bf16[16,1,192,640]{3,2,1,0:T(8,128)(2,1)} %get-tuple-element.107) | data formatting | bytes 7864320 | tf_op jit(solution)/shard_map/slice | solution.py:82
  321.0 9.8 %reshape_squeeze.14 = bf16[3072,5,128]{0,2,1:T(8,128)(2,1)} reshape(bf16[16,1,192,640]{2,0,3,1:T(8,128)(2,1)} %copy.86) | data formatting | bytes 7864320 | tf_op jit(solution)/shard_map/reshape;squeeze | solution.py:82
  335.9 9.0 %copy.90 = bf16[4608,5,128]{2,0,1:T(8,128)(2,1)} copy(bf16[4608,5,128]{0,2,1:T(8,128)(2,1)} %pad_maximum_fusion.2) | data formatting | bytes 11796480
  344.9 214.1 %while.11 = (s32[]{:T(128)}, bf16[6,256,5,128]{3,1,2,0:T(8,128)(2,1)S(1)}, bf16[6,256,5,128]{3,1,2,0:T(8,128)(2,1)}, bf16[4608,5,128]{2,0,1:T(8,128)(2,1)}, bf16...) while((s32[]{:T(128)}, bf16[6,256,5,128]{3,1,2,0:T(8,128)(2,1)S(1)}, ...), condition=%wide.region_11.12_spmd.clone, body=%wide.region_8.11_spmd.clone.sunk | while | flops 3085118464 | bytes 106874992 | solution.py:92
  344.9 13.8 %fusion.66 = (f32[5,256]{1,0:T(8,128)S(1)}, f32[5,256,4608]{2,1,0:T(8,128)}) fusion(pred[4608]{0:T(1024)(128)(4,1)S(1)} %fusion.65, bf16[4608,5,128]{2,0,1:T(8,128)(2,1)} %get-tuple-element.178, bf16[6,256,5,128]{3,1,2,0:T(8,128)(2,1)} %get-tuple-element.177, s32[]{:T(128)} %get-tuple-element.168), kind=kOutput, calls=%fused_computation.5.clone.1 | convolution fusion | flops 1527642880 | bytes 29829120 | tf_op jit(solution)/shard_map/while/body/eval_jaxpr/qhd,khd->hqk/dot_general | solution.py:18
  358.7 10.9 %fusion.67 = f32[5,256]{1,0:T(8,128)S(1)} fusion(f32[5,256,4608]{2,1,0:T(8,128)} %get-tuple-element.159, f32[5,256]{1,0:T(8,128)S(1)} %get-tuple-element.160, pred[4608]{0:T(1024)(128)(4,1)S(1)} %fusion.65), kind=kLoop, calls=%fused_computation.6.clone.1 | loop fusion | flops 23591680 | bytes 23607808 | tf_op jit(solution)/shard_map/while/body/eval_jaxpr/reduce_sum | solution.py:24
  369.7 10.9 %fusion.68 = bf16[6,256,5,128]{3,1,2,0:T(8,128)(2,1)S(1)} fusion(bf16[6,256,5,128]{3,1,2,0:T(8,128)(2,1)S(1)} %get-tuple-element.169, s32[]{:T(128)} %get-tuple-element.168, bf16[4608,5,128]{2,0,1:T(8,128)(2,1)S(1)} %copy-done.5, f32[5,256,4608]{2,1,0:T(8,128)} %get-tuple-element.159, f32[5,256]{1,0:T(8,128)S(1)} %get-tuple-element.160, ...), kind=kOutput, calls=%fused_computation.14.clone.1 | convolution fusion | flops 1533870080 | bytes 29840388 | tf_op jit(solution)/shard_map/while/body/eval_jaxpr/hqk,khd->qhd/dot_general | solution.py:25
  380.6 13.8 %fusion.66 = (f32[5,256]{1,0:T(8,128)S(1)}, f32[5,256,4608]{2,1,0:T(8,128)}) fusion(pred[4608]{0:T(1024)(128)(4,1)S(1)} %fusion.65, bf16[4608,5,128]{2,0,1:T(8,128)(2,1)} %get-tuple-element.178, bf16[6,256,5,128]{3,1,2,0:T(8,128)(2,1)} %get-tuple-element.177, s32[]{:T(128)} %get-tuple-element.168), kind=kOutput, calls=%fused_computation.5.clone.1 | convolution fusion | flops 1527642880 | bytes 29829120 | tf_op jit(solution)/shard_map/while/body/eval_jaxpr/qhd,khd->hqk/dot_general | solution.py:18
  394.4 10.9 %fusion.67 = f32[5,256]{1,0:T(8,128)S(1)} fusion(f32[5,256,4608]{2,1,0:T(8,128)} %get-tuple-element.159, f32[5,256]{1,0:T(8,128)S(1)} %get-tuple-element.160, pred[4608]{0:T(1024)(128)(4,1)S(1)} %fusion.65), kind=kLoop, calls=%fused_computation.6.clone.1 | loop fusion | flops 23591680 | bytes 23607808 | tf_op jit(solution)/shard_map/while/body/eval_jaxpr/reduce_sum | solution.py:24
  405.4 10.9 %fusion.68 = bf16[6,256,5,128]{3,1,2,0:T(8,128)(2,1)S(1)} fusion(bf16[6,256,5,128]{3,1,2,0:T(8,128)(2,1)S(1)} %get-tuple-element.169, s32[]{:T(128)} %get-tuple-element.168, bf16[4608,5,128]{2,0,1:T(8,128)(2,1)S(1)} %copy-done.5, f32[5,256,4608]{2,1,0:T(8,128)} %get-tuple-element.159, f32[5,256]{1,0:T(8,128)S(1)} %get-tuple-element.160, ...), kind=kOutput, calls=%fused_computation.14.clone.1 | convolution fusion | flops 1533870080 | bytes 29840388 | tf_op jit(solution)/shard_map/while/body/eval_jaxpr/hqk,khd->qhd/dot_general | solution.py:25
  416.3 13.8 %fusion.66 = (f32[5,256]{1,0:T(8,128)S(1)}, f32[5,256,4608]{2,1,0:T(8,128)}) fusion(pred[4608]{0:T(1024)(128)(4,1)S(1)} %fusion.65, bf16[4608,5,128]{2,0,1:T(8,128)(2,1)} %get-tuple-element.178, bf16[6,256,5,128]{3,1,2,0:T(8,128)(2,1)} %get-tuple-element.177, s32[]{:T(128)} %get-tuple-element.168), kind=kOutput, calls=%fused_computation.5.clone.1 | convolution fusion | flops 1527642880 | bytes 29829120 | tf_op jit(solution)/shard_map/while/body/eval_jaxpr/qhd,khd->hqk/dot_general | solution.py:18
  430.1 10.9 %fusion.67 = f32[5,256]{1,0:T(8,128)S(1)} fusion(f32[5,256,4608]{2,1,0:T(8,128)} %get-tuple-element.159, f32[5,256]{1,0:T(8,128)S(1)} %get-tuple-element.160, pred[4608]{0:T(1024)(128)(4,1)S(1)} %fusion.65), kind=kLoop, calls=%fused_computation.6.clone.1 | loop fusion | flops 23591680 | bytes 23607808 | tf_op jit(solution)/shard_map/while/body/eval_jaxpr/reduce_sum | solution.py:24
  441.1 10.9 %fusion.68 = bf16[6,256,5,128]{3,1,2,0:T(8,128)(2,1)S(1)} fusion(bf16[6,256,5,128]{3,1,2,0:T(8,128)(2,1)S(1)} %get-tuple-element.169, s32[]{:T(128)} %get-tuple-element.168, bf16[4608,5,128]{2,0,1:T(8,128)(2,1)S(1)} %copy-done.5, f32[5,256,4608]{2,1,0:T(8,128)} %get-tuple-element.159, f32[5,256]{1,0:T(8,128)S(1)} %get-tuple-element.160, ...), kind=kOutput, calls=%fused_computation.14.clone.1 | convolution fusion | flops 1533870080 | bytes 29840388 | tf_op jit(solution)/shard_map/while/body/eval_jaxpr/hqk,khd->qhd/dot_general | solution.py:25
  452.0 13.8 %fusion.66 = (f32[5,256]{1,0:T(8,128)S(1)}, f32[5,256,4608]{2,1,0:T(8,128)}) fusion(pred[4608]{0:T(1024)(128)(4,1)S(1)} %fusion.65, bf16[4608,5,128]{2,0,1:T(8,128)(2,1)} %get-tuple-element.178, bf16[6,256,5,128]{3,1,2,0:T(8,128)(2,1)} %get-tuple-element.177, s32[]{:T(128)} %get-tuple-element.168), kind=kOutput, calls=%fused_computation.5.clone.1 | convolution fusion | flops 1527642880 | bytes 29829120 | tf_op jit(solution)/shard_map/while/body/eval_jaxpr/qhd,khd->hqk/dot_general | solution.py:18
  465.8 10.9 %fusion.67 = f32[5,256]{1,0:T(8,128)S(1)} fusion(f32[5,256,4608]{2,1,0:T(8,128)} %get-tuple-element.159, f32[5,256]{1,0:T(8,128)S(1)} %get-tuple-element.160, pred[4608]{0:T(1024)(128)(4,1)S(1)} %fusion.65), kind=kLoop, calls=%fused_computation.6.clone.1 | loop fusion | flops 23591680 | bytes 23607808 | tf_op jit(solution)/shard_map/while/body/eval_jaxpr/reduce_sum | solution.py:24
  476.8 10.9 %fusion.68 = bf16[6,256,5,128]{3,1,2,0:T(8,128)(2,1)S(1)} fusion(bf16[6,256,5,128]{3,1,2,0:T(8,128)(2,1)S(1)} %get-tuple-element.169, s32[]{:T(128)} %get-tuple-element.168, bf16[4608,5,128]{2,0,1:T(8,128)(2,1)S(1)} %copy-done.5, f32[5,256,4608]{2,1,0:T(8,128)} %get-tuple-element.159, f32[5,256]{1,0:T(8,128)S(1)} %get-tuple-element.160, ...), kind=kOutput, calls=%fused_computation.14.clone.1 | convolution fusion | flops 1533870080 | bytes 29840388 | tf_op jit(solution)/shard_map/while/body/eval_jaxpr/hqk,khd->qhd/dot_general | solution.py:25
  487.6 13.8 %fusion.66 = (f32[5,256]{1,0:T(8,128)S(1)}, f32[5,256,4608]{2,1,0:T(8,128)}) fusion(pred[4608]{0:T(1024)(128)(4,1)S(1)} %fusion.65, bf16[4608,5,128]{2,0,1:T(8,128)(2,1)} %get-tuple-element.178, bf16[6,256,5,128]{3,1,2,0:T(8,128)(2,1)} %get-tuple-element.177, s32[]{:T(128)} %get-tuple-element.168), kind=kOutput, calls=%fused_computation.5.clone.1 | convolution fusion | flops 1527642880 | bytes 29829120 | tf_op jit(solution)/shard_map/while/body/eval_jaxpr/qhd,khd->hqk/dot_general | solution.py:18
  501.5 10.9 %fusion.67 = f32[5,256]{1,0:T(8,128)S(1)} fusion(f32[5,256,4608]{2,1,0:T(8,128)} %get-tuple-element.159, f32[5,256]{1,0:T(8,128)S(1)} %get-tuple-element.160, pred[4608]{0:T(1024)(128)(4,1)S(1)} %fusion.65), kind=kLoop, calls=%fused_computation.6.clone.1 | loop fusion | flops 23591680 | bytes 23607808 | tf_op jit(solution)/shard_map/while/body/eval_jaxpr/reduce_sum | solution.py:24
  512.4 10.9 %fusion.68 = bf16[6,256,5,128]{3,1,2,0:T(8,128)(2,1)S(1)} fusion(bf16[6,256,5,128]{3,1,2,0:T(8,128)(2,1)S(1)} %get-tuple-element.169, s32[]{:T(128)} %get-tuple-element.168, bf16[4608,5,128]{2,0,1:T(8,128)(2,1)S(1)} %copy-done.5, f32[5,256,4608]{2,1,0:T(8,128)} %get-tuple-element.159, f32[5,256]{1,0:T(8,128)S(1)} %get-tuple-element.160, ...), kind=kOutput, calls=%fused_computation.14.clone.1 | convolution fusion | flops 1533870080 | bytes 29840388 | tf_op jit(solution)/shard_map/while/body/eval_jaxpr/hqk,khd->qhd/dot_general | solution.py:25
  523.3 13.8 %fusion.66 = (f32[5,256]{1,0:T(8,128)S(1)}, f32[5,256,4608]{2,1,0:T(8,128)}) fusion(pred[4608]{0:T(1024)(128)(4,1)S(1)} %fusion.65, bf16[4608,5,128]{2,0,1:T(8,128)(2,1)} %get-tuple-element.178, bf16[6,256,5,128]{3,1,2,0:T(8,128)(2,1)} %get-tuple-element.177, s32[]{:T(128)} %get-tuple-element.168), kind=kOutput, calls=%fused_computation.5.clone.1 | convolution fusion | flops 1527642880 | bytes 29829120 | tf_op jit(solution)/shard_map/while/body/eval_jaxpr/qhd,khd->hqk/dot_general | solution.py:18
  537.2 10.9 %fusion.67 = f32[5,256]{1,0:T(8,128)S(1)} fusion(f32[5,256,4608]{2,1,0:T(8,128)} %get-tuple-element.159, f32[5,256]{1,0:T(8,128)S(1)} %get-tuple-element.160, pred[4608]{0:T(1024)(128)(4,1)S(1)} %fusion.65), kind=kLoop, calls=%fused_computation.6.clone.1 | loop fusion | flops 23591680 | bytes 23607808 | tf_op jit(solution)/shard_map/while/body/eval_jaxpr/reduce_sum | solution.py:24
  548.1 10.9 %fusion.68 = bf16[6,256,5,128]{3,1,2,0:T(8,128)(2,1)S(1)} fusion(bf16[6,256,5,128]{3,1,2,0:T(8,128)(2,1)S(1)} %get-tuple-element.169, s32[]{:T(128)} %get-tuple-element.168, bf16[4608,5,128]{2,0,1:T(8,128)(2,1)S(1)} %copy-done.5, f32[5,256,4608]{2,1,0:T(8,128)} %get-tuple-element.159, f32[5,256]{1,0:T(8,128)S(1)} %get-tuple-element.160, ...), kind=kOutput, calls=%fused_computation.14.clone.1 | convolution fusion | flops 1533870080 | bytes 29840388 | tf_op jit(solution)/shard_map/while/body/eval_jaxpr/hqk,khd->qhd/dot_general | solution.py:25
  566.6 29.3 %all_to_all.39 = bf16[8,192,640]{2,1,0:T(8,128)(2,1)S(1)} all-to-all(bf16[8,192,640]{2,1,0:T(8,128)(2,1)} %all_to_all.33), channel_id=1, replica_groups=mesh['wide'=8,'rep'=16] {'wide'}, dimensions={0} | all-to-all | bytes 3932160 | tf_op jit(solution)/shard_map/all_to_all | solution.py:94
  (74 shorter events, 86.5 us)
Async XLA Ops:
  0.0 30.1 %copy-start = (s32[16,16]{1,0:T(8,128)S(1)}, s32[16,16]{1,0:T(8,128)}, u32[]{:S(2)}) copy-start(s32[16,16]{1,0:T(8,128)} %param.12) | copy-start | bytes 3076
  0.0 4.9 copy-start.2
  0.0 4.8 copy-start.8
  24.8 5.3 copy-start.9
  24.8 122.3 %all-to-all-start = ((bf16[192,3,5120]{0,1,2:T(4,128)(2,1)}), bf16[192,3,5120]{0,1,2:T(4,128)(2,1)}, u32[]{:S(2)}, u32[]{:S(2)}) async-start(bf16[192,3,5120]{0,1,2:T(4,128)(2,1)} %copy.77), calls=%async_computation | async-start | bytes 20971520 | tf_op jit(solution)/shard_map/all_to_all | solution.py:42
  147.1 9.7 %copy-start.10 = (s32[16]{0:T(128)S(1)}, s32[16]{0:T(128)}, u32[]{:S(2)}) copy-start(s32[16]{0:T(128)} %param.11) | copy-start | bytes 196
  147.1 111.7 %all-to-all-start.1 = ((bf16[128,1,2,24,640]{4,3,2,1,0:T(8,128)(2,1)}), bf16[128,1,2,24,640]{4,3,2,1,0:T(8,128)(2,1)}, u32[]{:S(2)}, u32[]{:S(2)}) async-start(bf16[128,1,2,24,640]{4,3,2,1,0:T(8,128)(2,1)} %bitcast.97), calls=%async_computation.1 | async-start | bytes 15728640 | tf_op jit(solution)/shard_map/all_to_all | solution.py:61
  288.6 9.9 %copy-start.4 = (bf16[1536,1,640]{0,2,1:T(8,128)(2,1)S(1)}, bf16[1536,1,640]{0,2,1:T(8,128)(2,1)}, u32[]{:S(2)}) copy-start(bf16[1536,1,640]{0,2,1:T(8,128)(2,1)} %copy.85) | copy-start | bytes 5898244
  321.0 9.8 %copy-start.3 = (bf16[1536,1,640]{0,2,1:T(8,128)(2,1)S(1)}, bf16[1536,1,640]{0,2,1:T(8,128)(2,1)}, u32[]{:S(2)}) copy-start(bf16[1536,1,640]{0,2,1:T(8,128)(2,1)} %copy.87) | copy-start | bytes 5898244
  335.9 9.0 %copy-start.6 = (bf16[6,256,5,128]{3,1,2,0:T(8,128)(2,1)S(1)}, bf16[6,256,5,128]{3,1,2,0:T(8,128)(2,1)}, u32[]{:S(2)}) copy-start(bf16[6,256,5,128]{3,1,2,0:T(8,128)(2,1)} %custom-call.4) | copy-start | bytes 5898244
  358.7 10.9 %copy-start.5 = (bf16[4608,5,128]{2,0,1:T(8,128)(2,1)S(1)}, bf16[4608,5,128]{2,0,1:T(8,128)(2,1)}, u32[]{:S(2)}) copy-start(bf16[4608,5,128]{2,0,1:T(8,128)(2,1)} %get-tuple-element.179) | copy-start | bytes 17694724 | tf_op jit(solution)/shard_map/while
  394.4 10.9 %copy-start.5 = (bf16[4608,5,128]{2,0,1:T(8,128)(2,1)S(1)}, bf16[4608,5,128]{2,0,1:T(8,128)(2,1)}, u32[]{:S(2)}) copy-start(bf16[4608,5,128]{2,0,1:T(8,128)(2,1)} %get-tuple-element.179) | copy-start | bytes 17694724 | tf_op jit(solution)/shard_map/while
  430.1 10.9 %copy-start.5 = (bf16[4608,5,128]{2,0,1:T(8,128)(2,1)S(1)}, bf16[4608,5,128]{2,0,1:T(8,128)(2,1)}, u32[]{:S(2)}) copy-start(bf16[4608,5,128]{2,0,1:T(8,128)(2,1)} %get-tuple-element.179) | copy-start | bytes 17694724 | tf_op jit(solution)/shard_map/while
  465.8 10.9 %copy-start.5 = (bf16[4608,5,128]{2,0,1:T(8,128)(2,1)S(1)}, bf16[4608,5,128]{2,0,1:T(8,128)(2,1)}, u32[]{:S(2)}) copy-start(bf16[4608,5,128]{2,0,1:T(8,128)(2,1)} %get-tuple-element.179) | copy-start | bytes 17694724 | tf_op jit(solution)/shard_map/while
  501.5 10.9 %copy-start.5 = (bf16[4608,5,128]{2,0,1:T(8,128)(2,1)S(1)}, bf16[4608,5,128]{2,0,1:T(8,128)(2,1)}, u32[]{:S(2)}) copy-start(bf16[4608,5,128]{2,0,1:T(8,128)(2,1)} %get-tuple-element.179) | copy-start | bytes 17694724 | tf_op jit(solution)/shard_map/while
  537.2 10.9 %copy-start.5 = (bf16[4608,5,128]{2,0,1:T(8,128)(2,1)S(1)}, bf16[4608,5,128]{2,0,1:T(8,128)(2,1)}, u32[]{:S(2)}) copy-start(bf16[4608,5,128]{2,0,1:T(8,128)(2,1)} %get-tuple-element.179) | copy-start | bytes 17694724 | tf_op jit(solution)/shard_map/while
  559.0 1.3 copy-start.7
  563.2 36.1 %copy-start.1 = (s32[16,16]{1,0:T(8,128)S(1)}, s32[16,16]{1,0:T(8,128)}, u32[]{:S(2)}) copy-start(s32[16,16]{1,0:T(8,128)} %param.12) | copy-start | bytes 3076
where the time goes:
time: 602 us; the launch traced here: 599 us
  waiting for transfers between devices  166 us (28%)
  local copies, waits for them, and re-layouts  155 us (26%)
  matrix products  148 us (25%)
  other arithmetic  85.8 us (14%)
  blocking collectives  29.3 us (5%)
  starting transfers between devices  14.3 us (2%)
    all_to_all x1, waiting for transfers between devices, body(): lax.all_to_all(framed, 'wide', split_axis=2, concat_axis=0, tiled=True)  99.4 us
    dot_general x6, matrix products, attend_block(): jnp.einsum('qhd,khd->hqk', query_rows, all_keys, preferred_element_type=j...  83.1 us
    all_to_all x1, waiting for transfers between devices, body(): lax.all_to_all(moved, ('wide', 'rep'), split_axis=0, concat_axis=0, tiled...  66.4 us
    reduce_sum x6, other arithmetic, attend_block(): row_total = jnp.sum(weights, axis=-1, keepdims=True)  65.6 us
    dot_general x6, matrix products, attend_block(): jnp.einsum('hqk,khd->qhd', weights.astype(jnp.bfloat16), all_values, pref...  65.1 us
    all_to_all x1, blocking collectives, body(): lax.all_to_all(attended, 'wide', split_axis=0, concat_axis=1, tiled=True)  29.3 us
    unnamed x24, local copies, waits for them, and re-layouts  26 us
    all_to_all x1, local copies, waits for them, and re-layouts, body(): lax.all_to_all(framed, 'wide', split_axis=2, concat_axis=0, tiled=True)  15.7 us
  transfers between devices with their start and end apart: 2, of which 2 were waited for; matrix products, arithmetic and copies ran while one was open for 9% of the time, Pallas kernels for 0%

commit v1 on v0

--- a/solution.py
+++ b/solution.py
@@ -39,7 +39,10 @@
     queries = normalize(stretch_rows[:, 0], norm_gains[0])
     keys_new = normalize(stretch_rows[:, 1], norm_gains[1])
     framed = jnp.stack([queries, keys_new, stretch_rows[:, 2]], axis=1)
-    headed = lax.all_to_all(framed, "wide", split_axis=2, concat_axis=0, tiled=True)
+    headed = jnp.concatenate(
+        lax.all_to_all(jnp.stack(jnp.split(framed, lax.axis_size("wide"), axis=2)), "wide", 0, 0),
+        axis=0,
+    )
     stretch_len = headed.shape[0]
     slots_dev = cache.shape[0]
     cap_dev = slots_dev // rep_count

time: 602 us -> 542 us (0.900)
  waiting for transfers between devices: 166 us -> 132 us
  local copies, waits for them, and re-layouts: 155 us -> 132 us
    all_to_all x1, waiting for transfers between devices: 99.4 us -> 50.1 us  [body(): lax.all_to_all(jnp.stack(jnp.split(framed, lax.axis_size('wide'), axis=2)...]
    all_to_all x1, waiting for transfers between devices: 66.4 us -> 81.8 us  [body(): lax.all_to_all(moved, ('wide', 'rep'), split_axis=0, concat_axis=0, tiled...]
    another operation x1, local copies, waits for them, and re-layouts: 15.6 us -> 0.95 us  [body(): jnp.stack(jnp.split(framed, lax.axis_size('wide'), axis=2))]
    all_to_all x1, local copies, waits for them, and re-layouts: 15.7 us -> 3.21 us  [body(): lax.all_to_all(jnp.stack(jnp.split(framed, lax.axis_size('wide'), axis=2)...]
    unnamed x24 -> x31, local copies, waits for them, and re-layouts: 26 us -> 32.7 us
  transfers between devices with their start and end apart: 2 -> 2, of which waited for: 2 -> 2; matrix products, arithmetic and copies ran while one was open for 9% -> 7% of each run, Pallas kernels for 0% -> 0%
where the time goes in v1:
time: 542 us; the launch traced here: 540 us
  matrix products  148 us (27%)
  local copies, waits for them, and re-layouts  132 us (24%)
  waiting for transfers between devices  132 us (24%)
  other arithmetic  83.6 us (15%)
  blocking collectives  29.3 us (5%)
  starting transfers between devices  13.9 us (3%)
    dot_general x6, matrix products, attend_block(): jnp.einsum('qhd,khd->hqk', query_rows, all_keys, preferred_element_type=j...  83.1 us
    all_to_all x1, waiting for transfers between devices, body(): lax.all_to_all(moved, ('wide', 'rep'), split_axis=0, concat_axis=0, tiled...  81.8 us
    reduce_sum x6, other arithmetic, attend_block(): row_total = jnp.sum(weights, axis=-1, keepdims=True)  65.6 us
    dot_general x6, matrix products, attend_block(): jnp.einsum('hqk,khd->qhd', weights.astype(jnp.bfloat16), all_values, pref...  65.1 us
    all_to_all x1, waiting for transfers between devices, body(): lax.all_to_all(jnp.stack(jnp.split(framed, lax.axis_size('wide'), axis=2)...  50.1 us
    unnamed x31, local copies, waits for them, and re-layouts  32.7 us
    all_to_all x1, blocking collectives, body(): lax.all_to_all(attended, 'wide', split_axis=0, concat_axis=1, tiled=True)  29.3 us
    slice x2, local copies, waits for them, and re-layouts, body(): hist_values = history[:, 1].reshape(hist_span, heads_dev, HD)  14.1 us
  transfers between devices with their start and end apart: 2, of which 2 were waited for; matrix products, arithmetic and copies ran while one was open for 7% of the time, Pallas kernels for 0%

profile of v1, /device:TPU:8, one launch (start us, length us, event | category | flops | bytes accessed | tf_op | source)
XLA Modules:
  0.0 539.6 jit_solution(7226932671893427366)
XLA Ops:
  20.3 7.8 %gather_fusion = bf16[16,2,24,5120]{3,2,1,0:T(8,128)(2,1)} fusion(bf16[16,2,24,5120]{3,2,1,0:T(8,128)(2,1)} %param.10, s32[1024]{0:T(1024)S(1)} %get-tuple-element.115), kind=kCustom, calls=%fused_computation | custom fusion | bytes 15728704 | tf_op jit(solution)/shard_map/gather | solution.py:59
  37.4 50.1 %all-to-all-done = bf16[8,192,3,640]{3,1,2,0:T(8,128)(2,1)} async-done(((bf16[8,192,3,640]{3,1,2,0:T(8,128)(2,1)}), bf16[8,192,3,640]{3,1,2,0:T(8,128)(2,1)}, u32[]{:S(2)}, u32[]{:S(2)}) %all-to-all-start) | async-done | bytes 5898272 | tf_op jit(solution)/shard_map/all_to_all | solution.py:43
  87.4 9.0 %all-to-all-start.1 = ((bf16[128,1,2,24,640]{4,3,2,1,0:T(8,128)(2,1)}), bf16[128,1,2,24,640]{4,3,2,1,0:T(8,128)(2,1)}, u32[]{:S(2)}, u32[]{:S(2)}) async-start(bf16[128,1,2,24,640]{4,3,2,1,0:T(8,128)(2,1)} %bitcast.125), calls=%async_computation.1 | async-start | bytes 15728640 | tf_op jit(solution)/shard_map/all_to_all | solution.py:64
  117.3 81.8 %all-to-all-done.1 = bf16[128,1,2,24,640]{4,3,2,1,0:T(8,128)(2,1)} async-done(((bf16[128,1,2,24,640]{4,3,2,1,0:T(8,128)(2,1)}), bf16[128,1,2,24,640]{4,3,2,1,0:T(8,128)(2,1)}, u32[]{:S(2)}, u32[]{:S(2)}) %all-to-all-start.1) | async-done | bytes 7864352 | tf_op jit(solution)/shard_map/all_to_all | solution.py:64
  199.1 7.7 %copy.74 = bf16[16,1,2,8,24,640]{5,4,3,2,0,1:T(8,128)(2,1)} copy(bf16[16,1,2,8,24,640]{5,4,2,0,3,1:T(8,128)(2,1)} %bitcast.18) | data formatting | bytes 15728640 | tf_op jit(solution)/shard_map/transpose | solution.py:66
  206.8 8.0 %gather_fusion.1 = bf16[16,2,192,640]{3,2,1,0:T(8,128)(2,1)} fusion(bf16[16,2,192,640]{3,2,1,0:T(8,128)(2,1)} %bitcast.123, s32[1024]{0:T(1024)S(1)} %get-tuple-element.114), kind=kCustom, calls=%fused_computation.1 | custom fusion | bytes 15728704 | tf_op jit(solution)/shard_map/gather | solution.py:82
  220.4 8.5 %copy.75 = bf16[16,1,192,640]{2,0,3,1:T(8,128)(2,1)} copy(bf16[16,1,192,640]{3,2,1,0:T(8,128)(2,1)} %get-tuple-element.102) | data formatting | bytes 7864320 | tf_op jit(solution)/shard_map/slice | solution.py:84
  228.9 9.9 %reshape_squeeze.12 = bf16[3072,5,128]{0,2,1:T(8,128)(2,1)} reshape(bf16[16,1,192,640]{2,0,3,1:T(8,128)(2,1)} %copy.75) | data formatting | bytes 7864320 | tf_op jit(solution)/shard_map/reshape;squeeze | solution.py:84
  243.9 8.9 %copy.80 = bf16[4608,5,128]{2,0,1:T(8,128)(2,1)} copy(bf16[4608,5,128]{0,2,1:T(8,128)(2,1)} %pad_maximum_fusion.1) | data formatting | bytes 11796480
  252.7 8.5 %copy.77 = bf16[16,1,192,640]{2,0,3,1:T(8,128)(2,1)} copy(bf16[16,1,192,640]{3,2,1,0:T(8,128)(2,1)} %get-tuple-element.101) | data formatting | bytes 7864320 | tf_op jit(solution)/shard_map/slice | solution.py:85
  261.3 9.8 %reshape_squeeze.14 = bf16[3072,5,128]{0,2,1:T(8,128)(2,1)} reshape(bf16[16,1,192,640]{2,0,3,1:T(8,128)(2,1)} %copy.77) | data formatting | bytes 7864320 | tf_op jit(solution)/shard_map/reshape;squeeze | solution.py:85
  276.2 9.0 %copy.81 = bf16[4608,5,128]{2,0,1:T(8,128)(2,1)} copy(bf16[4608,5,128]{0,2,1:T(8,128)(2,1)} %pad_maximum_fusion.2) | data formatting | bytes 11796480
  285.2 214.1 %while.11 = (s32[]{:T(128)}, bf16[6,256,5,128]{3,1,2,0:T(8,128)(2,1)S(1)}, bf16[6,256,5,128]{3,1,2,0:T(8,128)(2,1)}, bf16[4608,5,128]{2,0,1:T(8,128)(2,1)}, bf16...) while((s32[]{:T(128)}, bf16[6,256,5,128]{3,1,2,0:T(8,128)(2,1)S(1)}, ...), condition=%wide.region_11.12_spmd.clone, body=%wide.region_8.11_spmd.clone.sunk | while | flops 3085118464 | bytes 106874992 | solution.py:95
  285.2 13.8 %fusion.74 = (f32[5,256]{1,0:T(8,128)S(1)}, f32[5,256,4608]{2,1,0:T(8,128)}) fusion(pred[4608]{0:T(1024)(128)(4,1)S(1)} %fusion.73, bf16[4608,5,128]{2,0,1:T(8,128)(2,1)} %get-tuple-element.174, bf16[6,256,5,128]{3,1,2,0:T(8,128)(2,1)} %get-tuple-element.173, s32[]{:T(128)} %get-tuple-element.164), kind=kOutput, calls=%fused_computation.5.clone.1 | convolution fusion | flops 1527642880 | bytes 29829120 | tf_op jit(solution)/shard_map/while/body/eval_jaxpr/qhd,khd->hqk/dot_general | solution.py:18
  299.0 10.9 %fusion.75 = f32[5,256]{1,0:T(8,128)S(1)} fusion(f32[5,256,4608]{2,1,0:T(8,128)} %get-tuple-element.155, f32[5,256]{1,0:T(8,128)S(1)} %get-tuple-element.156, pred[4608]{0:T(1024)(128)(4,1)S(1)} %fusion.73), kind=kLoop, calls=%fused_computation.6.clone.1 | loop fusion | flops 23591680 | bytes 23607808 | tf_op jit(solution)/shard_map/while/body/eval_jaxpr/reduce_sum | solution.py:24
  310.0 10.9 %fusion.76 = bf16[6,256,5,128]{3,1,2,0:T(8,128)(2,1)S(1)} fusion(bf16[6,256,5,128]{3,1,2,0:T(8,128)(2,1)S(1)} %get-tuple-element.165, s32[]{:T(128)} %get-tuple-element.164, bf16[4608,5,128]{2,0,1:T(8,128)(2,1)S(1)} %copy-done.5, f32[5,256,4608]{2,1,0:T(8,128)} %get-tuple-element.155, f32[5,256]{1,0:T(8,128)S(1)} %get-tuple-element.156, ...), kind=kOutput, calls=%fused_computation.14.clone.1 | convolution fusion | flops 1533870080 | bytes 29840388 | tf_op jit(solution)/shard_map/while/body/eval_jaxpr/hqk,khd->qhd/dot_general | solution.py:25
  320.9 13.8 %fusion.74 = (f32[5,256]{1,0:T(8,128)S(1)}, f32[5,256,4608]{2,1,0:T(8,128)}) fusion(pred[4608]{0:T(1024)(128)(4,1)S(1)} %fusion.73, bf16[4608,5,128]{2,0,1:T(8,128)(2,1)} %get-tuple-element.174, bf16[6,256,5,128]{3,1,2,0:T(8,128)(2,1)} %get-tuple-element.173, s32[]{:T(128)} %get-tuple-element.164), kind=kOutput, calls=%fused_computation.5.clone.1 | convolution fusion | flops 1527642880 | bytes 29829120 | tf_op jit(solution)/shard_map/while/body/eval_jaxpr/qhd,khd->hqk/dot_general | solution.py:18
  334.7 10.9 %fusion.75 = f32[5,256]{1,0:T(8,128)S(1)} fusion(f32[5,256,4608]{2,1,0:T(8,128)} %get-tuple-element.155, f32[5,256]{1,0:T(8,128)S(1)} %get-tuple-element.156, pred[4608]{0:T(1024)(128)(4,1)S(1)} %fusion.73), kind=kLoop, calls=%fused_computation.6.clone.1 | loop fusion | flops 23591680 | bytes 23607808 | tf_op jit(solution)/shard_map/while/body/eval_jaxpr/reduce_sum | solution.py:24
  345.6 10.9 %fusion.76 = bf16[6,256,5,128]{3,1,2,0:T(8,128)(2,1)S(1)} fusion(bf16[6,256,5,128]{3,1,2,0:T(8,128)(2,1)S(1)} %get-tuple-element.165, s32[]{:T(128)} %get-tuple-element.164, bf16[4608,5,128]{2,0,1:T(8,128)(2,1)S(1)} %copy-done.5, f32[5,256,4608]{2,1,0:T(8,128)} %get-tuple-element.155, f32[5,256]{1,0:T(8,128)S(1)} %get-tuple-element.156, ...), kind=kOutput, calls=%fused_computation.14.clone.1 | convolution fusion | flops 1533870080 | bytes 29840388 | tf_op jit(solution)/shard_map/while/body/eval_jaxpr/hqk,khd->qhd/dot_general | solution.py:25
  356.5 13.8 %fusion.74 = (f32[5,256]{1,0:T(8,128)S(1)}, f32[5,256,4608]{2,1,0:T(8,128)}) fusion(pred[4608]{0:T(1024)(128)(4,1)S(1)} %fusion.73, bf16[4608,5,128]{2,0,1:T(8,128)(2,1)} %get-tuple-element.174, bf16[6,256,5,128]{3,1,2,0:T(8,128)(2,1)} %get-tuple-element.173, s32[]{:T(128)} %get-tuple-element.164), kind=kOutput, calls=%fused_computation.5.clone.1 | convolution fusion | flops 1527642880 | bytes 29829120 | tf_op jit(solution)/shard_map/while/body/eval_jaxpr/qhd,khd->hqk/dot_general | solution.py:18
  370.4 10.9 %fusion.75 = f32[5,256]{1,0:T(8,128)S(1)} fusion(f32[5,256,4608]{2,1,0:T(8,128)} %get-tuple-element.155, f32[5,256]{1,0:T(8,128)S(1)} %get-tuple-element.156, pred[4608]{0:T(1024)(128)(4,1)S(1)} %fusion.73), kind=kLoop, calls=%fused_computation.6.clone.1 | loop fusion | flops 23591680 | bytes 23607808 | tf_op jit(solution)/shard_map/while/body/eval_jaxpr/reduce_sum | solution.py:24
  381.3 10.9 %fusion.76 = bf16[6,256,5,128]{3,1,2,0:T(8,128)(2,1)S(1)} fusion(bf16[6,256,5,128]{3,1,2,0:T(8,128)(2,1)S(1)} %get-tuple-element.165, s32[]{:T(128)} %get-tuple-element.164, bf16[4608,5,128]{2,0,1:T(8,128)(2,1)S(1)} %copy-done.5, f32[5,256,4608]{2,1,0:T(8,128)} %get-tuple-element.155, f32[5,256]{1,0:T(8,128)S(1)} %get-tuple-element.156, ...), kind=kOutput, calls=%fused_computation.14.clone.1 | convolution fusion | flops 1533870080 | bytes 29840388 | tf_op jit(solution)/shard_map/while/body/eval_jaxpr/hqk,khd->qhd/dot_general | solution.py:25
  392.2 13.8 %fusion.74 = (f32[5,256]{1,0:T(8,128)S(1)}, f32[5,256,4608]{2,1,0:T(8,128)}) fusion(pred[4608]{0:T(1024)(128)(4,1)S(1)} %fusion.73, bf16[4608,5,128]{2,0,1:T(8,128)(2,1)} %get-tuple-element.174, bf16[6,256,5,128]{3,1,2,0:T(8,128)(2,1)} %get-tuple-element.173, s32[]{:T(128)} %get-tuple-element.164), kind=kOutput, calls=%fused_computation.5.clone.1 | convolution fusion | flops 1527642880 | bytes 29829120 | tf_op jit(solution)/shard_map/while/body/eval_jaxpr/qhd,khd->hqk/dot_general | solution.py:18
  406.1 10.9 %fusion.75 = f32[5,256]{1,0:T(8,128)S(1)} fusion(f32[5,256,4608]{2,1,0:T(8,128)} %get-tuple-element.155, f32[5,256]{1,0:T(8,128)S(1)} %get-tuple-element.156, pred[4608]{0:T(1024)(128)(4,1)S(1)} %fusion.73), kind=kLoop, calls=%fused_computation.6.clone.1 | loop fusion | flops 23591680 | bytes 23607808 | tf_op jit(solution)/shard_map/while/body/eval_jaxpr/reduce_sum | solution.py:24
  417.0 10.9 %fusion.76 = bf16[6,256,5,128]{3,1,2,0:T(8,128)(2,1)S(1)} fusion(bf16[6,256,5,128]{3,1,2,0:T(8,128)(2,1)S(1)} %get-tuple-element.165, s32[]{:T(128)} %get-tuple-element.164, bf16[4608,5,128]{2,0,1:T(8,128)(2,1)S(1)} %copy-done.5, f32[5,256,4608]{2,1,0:T(8,128)} %get-tuple-element.155, f32[5,256]{1,0:T(8,128)S(1)} %get-tuple-element.156, ...), kind=kOutput, calls=%fused_computation.14.clone.1 | convolution fusion | flops 1533870080 | bytes 29840388 | tf_op jit(solution)/shard_map/while/body/eval_jaxpr/hqk,khd->qhd/dot_general | solution.py:25
  427.9 13.8 %fusion.74 = (f32[5,256]{1,0:T(8,128)S(1)}, f32[5,256,4608]{2,1,0:T(8,128)}) fusion(pred[4608]{0:T(1024)(128)(4,1)S(1)} %fusion.73, bf16[4608,5,128]{2,0,1:T(8,128)(2,1)} %get-tuple-element.174, bf16[6,256,5,128]{3,1,2,0:T(8,128)(2,1)} %get-tuple-element.173, s32[]{:T(128)} %get-tuple-element.164), kind=kOutput, calls=%fused_computation.5.clone.1 | convolution fusion | flops 1527642880 | bytes 29829120 | tf_op jit(solution)/shard_map/while/body/eval_jaxpr/qhd,khd->hqk/dot_general | solution.py:18
  441.8 10.9 %fusion.75 = f32[5,256]{1,0:T(8,128)S(1)} fusion(f32[5,256,4608]{2,1,0:T(8,128)} %get-tuple-element.155, f32[5,256]{1,0:T(8,128)S(1)} %get-tuple-element.156, pred[4608]{0:T(1024)(128)(4,1)S(1)} %fusion.73), kind=kLoop, calls=%fused_computation.6.clone.1 | loop fusion | flops 23591680 | bytes 23607808 | tf_op jit(solution)/shard_map/while/body/eval_jaxpr/reduce_sum | solution.py:24
  452.7 10.9 %fusion.76 = bf16[6,256,5,128]{3,1,2,0:T(8,128)(2,1)S(1)} fusion(bf16[6,256,5,128]{3,1,2,0:T(8,128)(2,1)S(1)} %get-tuple-element.165, s32[]{:T(128)} %get-tuple-element.164, bf16[4608,5,128]{2,0,1:T(8,128)(2,1)S(1)} %copy-done.5, f32[5,256,4608]{2,1,0:T(8,128)} %get-tuple-element.155, f32[5,256]{1,0:T(8,128)S(1)} %get-tuple-element.156, ...), kind=kOutput, calls=%fused_computation.14.clone.1 | convolution fusion | flops 1533870080 | bytes 29840388 | tf_op jit(solution)/shard_map/while/body/eval_jaxpr/hqk,khd->qhd/dot_general | solution.py:25
  463.6 13.8 %fusion.74 = (f32[5,256]{1,0:T(8,128)S(1)}, f32[5,256,4608]{2,1,0:T(8,128)}) fusion(pred[4608]{0:T(1024)(128)(4,1)S(1)} %fusion.73, bf16[4608,5,128]{2,0,1:T(8,128)(2,1)} %get-tuple-element.174, bf16[6,256,5,128]{3,1,2,0:T(8,128)(2,1)} %get-tuple-element.173, s32[]{:T(128)} %get-tuple-element.164), kind=kOutput, calls=%fused_computation.5.clone.1 | convolution fusion | flops 1527642880 | bytes 29829120 | tf_op jit(solution)/shard_map/while/body/eval_jaxpr/qhd,khd->hqk/dot_general | solution.py:18
  477.5 10.9 %fusion.75 = f32[5,256]{1,0:T(8,128)S(1)} fusion(f32[5,256,4608]{2,1,0:T(8,128)} %get-tuple-element.155, f32[5,256]{1,0:T(8,128)S(1)} %get-tuple-element.156, pred[4608]{0:T(1024)(128)(4,1)S(1)} %fusion.73), kind=kLoop, calls=%fused_computation.6.clone.1 | loop fusion | flops 23591680 | bytes 23607808 | tf_op jit(solution)/shard_map/while/body/eval_jaxpr/reduce_sum | solution.py:24
  488.4 10.9 %fusion.76 = bf16[6,256,5,128]{3,1,2,0:T(8,128)(2,1)S(1)} fusion(bf16[6,256,5,128]{3,1,2,0:T(8,128)(2,1)S(1)} %get-tuple-element.165, s32[]{:T(128)} %get-tuple-element.164, bf16[4608,5,128]{2,0,1:T(8,128)(2,1)S(1)} %copy-done.5, f32[5,256,4608]{2,1,0:T(8,128)} %get-tuple-element.155, f32[5,256]{1,0:T(8,128)S(1)} %get-tuple-element.156, ...), kind=kOutput, calls=%fused_computation.14.clone.1 | convolution fusion | flops 1533870080 | bytes 29840388 | tf_op jit(solution)/shard_map/while/body/eval_jaxpr/hqk,khd->qhd/dot_general | solution.py:25
  506.9 29.3 %all_to_all.26 = bf16[8,192,640]{2,1,0:T(8,128)(2,1)S(1)} all-to-all(bf16[8,192,640]{2,1,0:T(8,128)(2,1)} %all_to_all.20), channel_id=1, replica_groups=mesh['wide'=8,'rep'=16] {'wide'}, dimensions={0} | all-to-all | bytes 3932160 | tf_op jit(solution)/shard_map/all_to_all | solution.py:97
  (80 shorter events, 76.5 us)
Async XLA Ops:
  0.0 19.5 %copy-start = (s32[16,16]{1,0:T(8,128)S(1)}, s32[16,16]{1,0:T(8,128)}, u32[]{:S(2)}) copy-start(s32[16,16]{1,0:T(8,128)} %param.12) | copy-start | bytes 3076
  0.0 4.9 copy-start.2
  0.0 4.8 copy-start.8
  14.6 4.9 copy-start.9
  14.6 72.8 %all-to-all-start = ((bf16[8,192,3,640]{3,1,2,0:T(8,128)(2,1)}), bf16[8,192,3,640]{3,1,2,0:T(8,128)(2,1)}, u32[]{:S(2)}, u32[]{:S(2)}) async-start(bf16[8,192,3,640]{3,1,2,0:T(8,128)(2,1)} %fusion.36), calls=%async_computation | async-start | bytes 11796480 | tf_op jit(solution)/shard_map/all_to_all | solution.py:43
  87.4 9.7 %copy-start.10 = (s32[16]{0:T(128)S(1)}, s32[16]{0:T(128)}, u32[]{:S(2)}) copy-start(s32[16]{0:T(128)} %param.11) | copy-start | bytes 196
  87.4 111.7 %all-to-all-start.1 = ((bf16[128,1,2,24,640]{4,3,2,1,0:T(8,128)(2,1)}), bf16[128,1,2,24,640]{4,3,2,1,0:T(8,128)(2,1)}, u32[]{:S(2)}, u32[]{:S(2)}) async-start(bf16[128,1,2,24,640]{4,3,2,1,0:T(8,128)(2,1)} %bitcast.125), calls=%async_computation.1 | async-start | bytes 15728640 | tf_op jit(solution)/shard_map/all_to_all | solution.py:64
  228.9 9.9 %copy-start.4 = (bf16[1536,1,640]{0,2,1:T(8,128)(2,1)S(1)}, bf16[1536,1,640]{0,2,1:T(8,128)(2,1)}, u32[]{:S(2)}) copy-start(bf16[1536,1,640]{0,2,1:T(8,128)(2,1)} %copy.76) | copy-start | bytes 5898244
  261.3 9.8 %copy-start.3 = (bf16[1536,1,640]{0,2,1:T(8,128)(2,1)S(1)}, bf16[1536,1,640]{0,2,1:T(8,128)(2,1)}, u32[]{:S(2)}) copy-start(bf16[1536,1,640]{0,2,1:T(8,128)(2,1)} %copy.78) | copy-start | bytes 5898244
  276.2 9.0 %copy-start.6 = (bf16[6,256,5,128]{3,1,2,0:T(8,128)(2,1)S(1)}, bf16[6,256,5,128]{3,1,2,0:T(8,128)(2,1)}, u32[]{:S(2)}) copy-start(bf16[6,256,5,128]{3,1,2,0:T(8,128)(2,1)} %custom-call.5) | copy-start | bytes 5898244
  299.0 10.9 %copy-start.5 = (bf16[4608,5,128]{2,0,1:T(8,128)(2,1)S(1)}, bf16[4608,5,128]{2,0,1:T(8,128)(2,1)}, u32[]{:S(2)}) copy-start(bf16[4608,5,128]{2,0,1:T(8,128)(2,1)} %get-tuple-element.175) | copy-start | bytes 17694724 | tf_op jit(solution)/shard_map/while
  334.7 10.9 %copy-start.5 = (bf16[4608,5,128]{2,0,1:T(8,128)(2,1)S(1)}, bf16[4608,5,128]{2,0,1:T(8,128)(2,1)}, u32[]{:S(2)}) copy-start(bf16[4608,5,128]{2,0,1:T(8,128)(2,1)} %get-tuple-element.175) | copy-start | bytes 17694724 | tf_op jit(solution)/shard_map/while
  370.4 10.9 %copy-start.5 = (bf16[4608,5,128]{2,0,1:T(8,128)(2,1)S(1)}, bf16[4608,5,128]{2,0,1:T(8,128)(2,1)}, u32[]{:S(2)}) copy-start(bf16[4608,5,128]{2,0,1:T(8,128)(2,1)} %get-tuple-element.175) | copy-start | bytes 17694724 | tf_op jit(solution)/shard_map/while
  406.1 10.9 %copy-start.5 = (bf16[4608,5,128]{2,0,1:T(8,128)(2,1)S(1)}, bf16[4608,5,128]{2,0,1:T(8,128)(2,1)}, u32[]{:S(2)}) copy-start(bf16[4608,5,128]{2,0,1:T(8,128)(2,1)} %get-tuple-element.175) | copy-start | bytes 17694724 | tf_op jit(solution)/shard_map/while
  441.8 10.9 %copy-start.5 = (bf16[4608,5,128]{2,0,1:T(8,128)(2,1)S(1)}, bf16[4608,5,128]{2,0,1:T(8,128)(2,1)}, u32[]{:S(2)}) copy-start(bf16[4608,5,128]{2,0,1:T(8,128)(2,1)} %get-tuple-element.175) | copy-start | bytes 17694724 | tf_op jit(solution)/shard_map/while
  477.5 10.9 %copy-start.5 = (bf16[4608,5,128]{2,0,1:T(8,128)(2,1)S(1)}, bf16[4608,5,128]{2,0,1:T(8,128)(2,1)}, u32[]{:S(2)}) copy-start(bf16[4608,5,128]{2,0,1:T(8,128)(2,1)} %get-tuple-element.175) | copy-start | bytes 17694724 | tf_op jit(solution)/shard_map/while
  499.3 1.3 copy-start.7
  503.5 36.1 %copy-start.1 = (s32[16,16]{1,0:T(8,128)S(1)}, s32[16,16]{1,0:T(8,128)}, u32[]{:S(2)}) copy-start(s32[16,16]{1,0:T(8,128)} %param.12) | copy-start | bytes 3076
